TPU v7x, 512 devices: a whole 4x4x16 slice. The times are simulated.
512 devices in a mesh: dp: 64 (over z, y), sub: 8 (over x, core).
Axes of the slice: x: 4, y: 4, z: 16, core: 2. Of those that a mesh axis runs over, the one named last changes fastest.
Arguments:
- embeddings: bfloat16 [524288, 1024], P(('dp', 'sub')), may hold values from -6 to 6
- cluster_of: int32 [524288], P(('dp', 'sub')), may hold values from 0 to 1087, as said below
Outputs:
- density: float32 [524288], P(('dp', 'sub'))
Inputs may be any that keep to these rules, and one draw needn't show every extreme that they name: `cluster_of`: A cluster c < 2 * 512 is held whole by the device of dp index (c // 2) // 8 and sub index (c // 2) % 8; a cluster c >= 2 * 512 is spread over the sub devices of dp index (c - 2 * 512). Of one device's rows exactly 896 lie in whole-held clusters and 128 in spread ones. At most 3 of one device's rows lie in the whole-held clusters of one device; one device gets exactly 3 such rows from every device. At most 4 of one device's rows lie in the spread clusters of one dp index; one dp index gets exactly 4 such rows from every device.
All inputs are finite; a program needn't handle non-finite values.
Results may differ from a plain program's by a relative error of at most 0.0005.
The roundings to bfloat16 on the way count: a program that leaves them out, or rounds other values in their place, can miss the bound.
Values may be sent and summed in bfloat16 or wider, within the bound.
A program may use at most 64 MiB of HBM per device.

v0:
```python
import jax
import jax.numpy as jnp
from jax import lax
from jax.sharding import PartitionSpec as P

SC = 2
LC = 1
kernel_scale = 32.0


def unit_norm(values):
    floats = values.astype(jnp.float32)
    scaled = floats * lax.rsqrt(jnp.sum(floats * floats, axis=1, keepdims=True) + 1e-06)
    return scaled.astype(jnp.bfloat16)


def pair_terms(left_rows, left_ids, left_place, right_rows, right_ids, right_place):
    similar = lax.dot_general(
        left_rows, right_rows, (((1,), (1,)), ((), ())), preferred_element_type=jnp.float32
    )
    same_cluster = (left_ids[:, None] == right_ids[None, :]) & (left_ids[:, None] >= 0)
    keep_pair = same_cluster & (left_place[:, None] != right_place[None, :])
    weights = jnp.where(keep_pair, jnp.exp(kernel_scale * similar), 0.0)
    return (weights, same_cluster.astype(jnp.float32))


def rank_within(labels):
    length = labels.shape[0]
    places = jnp.arange(length, dtype=jnp.int32)
    earlier = places[None, :] < places[:, None]
    matches = (labels[:, None] == labels[None, :]) & earlier
    return jnp.sum(matches.astype(jnp.int32), axis=1)


def finish(kernel_mass, members, labels):
    return jnp.where(labels >= 0, kernel_mass / jnp.maximum(members, 1.0), 0.0)


def local(embeddings, cluster_of):
    dp_count = lax.axis_size("dp")
    sub_count = lax.axis_size("sub")
    device_count = dp_count * sub_count
    local_rows = embeddings.shape[0]
    feature_width = embeddings.shape[1]
    spread_count = local_rows // 8
    planned_count = local_rows - spread_count
    small_cap = max(2, (3 * planned_count + 2 * device_count - 1) // (2 * device_count))
    large_cap = max(2, (2 * spread_count + dp_count - 1) // dp_count)
    unit_rows = unit_norm(embeddings)
    whole_count = SC * device_count
    planned = cluster_of < whole_count
    holder_of = cluster_of // SC
    owners = jnp.where(planned, holder_of // sub_count, (cluster_of - whole_count) // LC)
    tile_of = jnp.where(planned, holder_of % sub_count, -1)
    target = owners * sub_count + tile_of
    small_label = jnp.where(planned, target, -1)
    large_label = jnp.where(planned, -1, owners)
    small_slot = jnp.where(
        planned, target * small_cap + rank_within(small_label), device_count * small_cap
    )
    large_slot = jnp.where(
        planned, dp_count * large_cap, owners * large_cap + rank_within(large_label)
    )
    small_send = (
        jnp.zeros((device_count * small_cap, feature_width), jnp.bfloat16)
        .at[small_slot]
        .set(unit_rows, mode="drop")
    )
    small_send = small_send.reshape(dp_count, sub_count, small_cap, feature_width)
    small_tags = (
        jnp.full((device_count * small_cap,), -1, jnp.int32)
        .at[small_slot]
        .set(cluster_of, mode="drop")
    )
    small_tags = small_tags.reshape(dp_count, sub_count, small_cap)
    large_send = (
        jnp.zeros((dp_count * large_cap, feature_width), jnp.bfloat16)
        .at[large_slot]
        .set(unit_rows, mode="drop")
    )
    large_send = large_send.reshape(dp_count, large_cap, feature_width)
    large_tags = (
        jnp.full((dp_count * large_cap,), -1, jnp.int32).at[large_slot].set(cluster_of, mode="drop")
    )
    large_tags = large_tags.reshape(dp_count, large_cap)
    got_rows, got_tags = (
        lax.all_to_all(
            lax.all_to_all(small_send, "dp", split_axis=0, concat_axis=0, tiled=True),
            "sub",
            split_axis=1,
            concat_axis=1,
            tiled=True,
        ),
        lax.all_to_all(
            lax.all_to_all(small_tags, "dp", split_axis=0, concat_axis=0, tiled=True),
            "sub",
            split_axis=1,
            concat_axis=1,
            tiled=True,
        ),
    )
    got_large, got_large_tags = (
        lax.all_to_all(large_send, "dp", split_axis=0, concat_axis=0, tiled=True),
        lax.all_to_all(large_tags, "dp", split_axis=0, concat_axis=0, tiled=True),
    )
    planned_flat = got_rows.reshape(-1, feature_width)
    planned_ids = got_tags.reshape(-1)
    slot_total = planned_flat.shape[0]
    block_size = 512
    all_places = jnp.arange(slot_total, dtype=jnp.int32)

    def planned_block(block_index):
        block_start = block_index * block_size
        part_rows = lax.dynamic_slice_in_dim(planned_flat, block_start, block_size, 0)
        part_ids = lax.dynamic_slice_in_dim(planned_ids, block_start, block_size, 0)
        part_places = block_start + jnp.arange(block_size, dtype=jnp.int32)
        weights, same_cluster = pair_terms(
            part_rows, part_ids, part_places, planned_flat, planned_ids, all_places
        )
        return finish(jnp.sum(weights, axis=1), jnp.sum(same_cluster, axis=1), part_ids)

    planned_density = lax.map(planned_block, jnp.arange(slot_total // block_size, dtype=jnp.int32))
    planned_density = planned_density.reshape(dp_count, sub_count, small_cap)
    spread_flat = got_large.reshape(-1, feature_width)
    spread_ids = got_large_tags.reshape(-1)
    spread_total = spread_flat.shape[0]
    places = jnp.arange(spread_total, dtype=jnp.int32)
    my_places = lax.axis_index("sub") * spread_total + places
    piece_rows = lax.all_gather(spread_flat, "sub", axis=0, tiled=True)
    piece_ids = lax.all_gather(spread_ids, "sub", axis=0, tiled=True)
    piece_places = jnp.arange(piece_rows.shape[0], dtype=jnp.int32)
    weights, same_cluster = pair_terms(
        spread_flat, spread_ids, my_places, piece_rows, piece_ids, piece_places
    )
    kernel_mass = jnp.sum(weights, axis=1)
    members = jnp.sum(same_cluster, axis=1)
    spread_density = finish(kernel_mass, members, spread_ids).reshape(dp_count, large_cap)
    back_planned = lax.all_to_all(
        lax.all_to_all(planned_density, "dp", split_axis=0, concat_axis=0, tiled=True),
        "sub",
        split_axis=1,
        concat_axis=1,
        tiled=True,
    )
    back_spread = lax.all_to_all(spread_density, "dp", split_axis=0, concat_axis=0, tiled=True)
    from_planned = jnp.take(back_planned.reshape(-1), small_slot, mode="clip")
    from_spread = jnp.take(back_spread.reshape(-1), large_slot, mode="clip")
    return jnp.where(planned, from_planned, from_spread)


def solution(mesh):
    placed = (P(("dp", "sub"), None), P(("dp", "sub")))
    return jax.shard_map(
        local, mesh=mesh, in_specs=placed, out_specs=P(("dp", "sub")), check_vma=False
    )
```

profile of v0, /device:TPU:1, one launch (start us, length us, event | category | flops | bytes accessed | tf_op | source)
XLA Modules:
  0.0 422.4 jit_solution(3138771682105180316)
XLA Ops:
  13.8 19.3 %all-to-all-start.6 = ((s32[64,1,4]{2,1,0:T(1,128)}), s32[64,1,4]{2,1,0:T(1,128)S(1)}, u32[]{:S(2)}, u32[]{:S(2)}) async-start(s32[64,1,4]{2,1,0:T(1,128)} %bitcast), calls=%async_computation.6 | async-start | bytes 65536 | tf_op jit(solution)/shard_map/all_to_all | solution.py:104
  41.5 5.2 %all-to-all-done.6 = s32[64,1,4]{2,1,0:T(1,128)S(1)} async-done(((s32[64,1,4]{2,1,0:T(1,128)}), s32[64,1,4]{2,1,0:T(1,128)S(1)}, u32[]{:S(2)}, u32[]{:S(2)}) %all-to-all-start.6) | async-done | bytes 1056 | tf_op jit(solution)/shard_map/all_to_all | solution.py:104
  46.7 9.3 %all-to-all-start = ((s32[64,8,3]{1,2,0:T(4,128)}), s32[64,8,3]{1,2,0:T(4,128)S(1)}, u32[]{:S(2)}, u32[]{:S(2)}) async-start(s32[64,8,3]{1,2,0:T(4,128)} %copy.16), calls=%async_computation | async-start | bytes 262144 | tf_op jit(solution)/shard_map/all_to_all | solution.py:95
  56.0 5.7 %scatter_custom_fusion.3 = bf16[256,1024]{1,0:T(8,128)(2,1)S(1)} fusion(s32[1024]{0:T(1024)S(1)} %get-tuple-element.88, bf16[1024,1024]{1,0:T(8,128)(2,1)S(1)} %copy-done, f32[1024]{0:T(1024)S(1)} %add_rsqrt_fusion, bf16[]{:T(256)} %constant.90.clone.1), kind=kCustom, calls=%fused_computation.40 | custom fusion | flops 3145728 | bytes 2625538 | tf_op jit(solution)/shard_map/scatter | solution.py:79
  62.7 8.4 %all-to-all-done = s32[64,8,3]{1,2,0:T(4,128)S(1)} async-done(((s32[64,8,3]{1,2,0:T(4,128)}), s32[64,8,3]{1,2,0:T(4,128)S(1)}, u32[]{:S(2)}, u32[]{:S(2)}) %all-to-all-start) | async-done | bytes 6176 | tf_op jit(solution)/shard_map/all_to_all | solution.py:95
  71.1 6.4 %all-to-all-start.7 = ((bf16[64,4,1024]{2,1,0:T(4,128)(2,1)}), bf16[64,4,1024]{2,1,0:T(4,128)(2,1)S(1)}, u32[]{:S(2)}, u32[]{:S(2)}) async-start(bf16[64,4,1024]{2,1,0:T(4,128)(2,1)} %reshape.104), calls=%async_computation.7 | async-start | bytes 1048576 | tf_op jit(solution)/shard_map/all_to_all | solution.py:103
  77.5 7.8 %scatter_custom_fusion.1 = bf16[1536,1024]{1,0:T(8,128)(2,1)} fusion(s32[1024]{0:T(1024)S(1)} %get-tuple-element.90, bf16[]{:T(256)} %constant.90.clone.1, bf16[1024,1024]{1,0:T(8,128)(2,1)S(1)} %copy-done, f32[1024]{0:T(1024)S(1)} %add_rsqrt_fusion), kind=kCustom, calls=%fused_computation.37 | custom fusion | flops 3145728 | bytes 5246978 | tf_op jit(solution)/shard_map/scatter | solution.py:67
  85.3 9.1 %reshape.100 = bf16[64,8,3,1024]{3,2,1,0:T(4,128)(2,1)} reshape(bf16[1536,1024]{1,0:T(8,128)(2,1)} %scatter_custom_fusion.1) | data formatting | bytes 6291456 | tf_op jit(solution)/shard_map/reshape | solution.py:69
  94.4 5.6 %copy.19 = bf16[64,8,3,1024]{3,1,2,0:T(8,128)(2,1)} copy(bf16[64,8,3,1024]{3,2,1,0:T(4,128)(2,1)} %reshape.100) | data formatting | bytes 6291456 | tf_op jit(solution)/shard_map/reshape | solution.py:69
  100.0 6.3 %all-to-all-done.7 = bf16[64,4,1024]{2,1,0:T(4,128)(2,1)S(1)} async-done(((bf16[64,4,1024]{2,1,0:T(4,128)(2,1)}), bf16[64,4,1024]{2,1,0:T(4,128)(2,1)S(1)}, u32[]{:S(2)}, u32[]{:S(2)}) %all-to-all-start.7) | async-done | bytes 524320 | tf_op jit(solution)/shard_map/all_to_all | solution.py:103
  107.0 8.9 %all-to-all-start.2 = ((bf16[64,8,3,1024]{3,1,2,0:T(8,128)(2,1)}), bf16[64,8,3,1024]{3,1,2,0:T(8,128)(2,1)S(1)}, u32[]{:S(2)}, u32[]{:S(2)}) async-start(bf16[64,8,3,1024]{3,1,2,0:T(8,128)(2,1)} %copy.19), calls=%async_computation.2 | async-start | bytes 6291456 | tf_op jit(solution)/shard_map/all_to_all | solution.py:88
  118.8 135.5 %all-to-all-done.2 = bf16[64,8,3,1024]{3,1,2,0:T(8,128)(2,1)S(1)} async-done(((bf16[64,8,3,1024]{3,1,2,0:T(8,128)(2,1)}), bf16[64,8,3,1024]{3,1,2,0:T(8,128)(2,1)S(1)}, u32[]{:S(2)}, u32[]{:S(2)}) %all-to-all-start.2) | async-done | bytes 3145760 | tf_op jit(solution)/shard_map/all_to_all | solution.py:88
  254.3 12.1 %all-to-all-start.1 = ((s32[8,1,192]{2,1,0:T(1,128)}), s32[8,1,192]{2,1,0:T(1,128)S(1)}, u32[]{:S(2)}, u32[]{:S(2)}) async-start(s32[8,1,192]{2,1,0:T(1,128)} %reshape.193), calls=%async_computation.1 | async-start | bytes 16384 | tf_op jit(solution)/shard_map/all_to_all | solution.py:94
  276.7 39.7 %all-gather = s32[8,1,256]{2,1,0:T(1,128)S(1)} all-gather(s32[1,1,256]{2,1,0:T(1,128)S(1)} %reshape.161), channel_id=1, replica_groups=mesh['dp'=64,'sub'=8] {'sub'}, dimensions={0}, use_global_device_ids=true | all-gather | bytes 9216 | tf_op jit(solution)/shard_map/all_gather | solution.py:130
  323.3 4.6 %copy.21 = bf16[64,8,3,1024]{3,2,1,0:T(4,128)(2,1)} copy(bf16[64,8,3,1024]{3,0,2,1:T(8,128)(2,1)S(1)} %all-to-all-done.3) | data formatting | bytes 6291456 | tf_op jit(solution)/shard_map/all_to_all | solution.py:87
  327.9 7.5 %reshape.101 = bf16[1536,1024]{1,0:T(8,128)(2,1)S(1)} reshape(bf16[64,8,3,1024]{3,2,1,0:T(4,128)(2,1)} %copy.21) | data formatting | bytes 6291456 | tf_op jit(solution)/shard_map/reshape | solution.py:106
  335.4 15.6 %while.12 = (s32[]{:T(128)}, f32[3,512]{1,0:T(4,128)S(1)}, s32[3]{0:T(128)S(1)}, s32[1536]{0:T(1024)S(1)}, s32[64,8,3]{2,1,0:T(8,128)}, /*index=5*/bf16[1536,102...) while((s32[]{:T(128)}, f32[3,512]{1,0:T(4,128)S(1)}, ...), condition=%wide.wide.region_7.8_spmd.clone, body=%wide.wide.region_4.7_spmd.clone.sunk | while | flops 1619265024 | bytes 4237495 | solution.py:122
  352.3 5.6 %all-to-all-start.4 = ((f32[64,8,3]{1,2,0:T(4,128)}), f32[64,8,3]{1,2,0:T(4,128)S(1)}, u32[]{:S(2)}, u32[]{:S(2)}) async-start(f32[64,8,3]{1,2,0:T(4,128)} %copy.23), calls=%async_computation.4 | async-start | bytes 262144 | tf_op jit(solution)/shard_map/all_to_all | solution.py:139
  358.5 15.0 %all-to-all-done.4 = f32[64,8,3]{1,2,0:T(4,128)S(1)} async-done(((f32[64,8,3]{1,2,0:T(4,128)}), f32[64,8,3]{1,2,0:T(4,128)S(1)}, u32[]{:S(2)}, u32[]{:S(2)}) %all-to-all-start.4) | async-done | bytes 6176 | tf_op jit(solution)/shard_map/all_to_all | solution.py:139
  373.5 5.8 %all-to-all-start.8 = ((f32[64,1,4]{2,1,0:T(1,128)}), f32[64,1,4]{2,1,0:T(1,128)S(1)}, u32[]{:S(2)}, u32[]{:S(2)}) async-start(f32[64,1,4]{2,1,0:T(1,128)} %bitcast.3), calls=%async_computation.8 | async-start | bytes 65536 | tf_op jit(solution)/shard_map/all_to_all | solution.py:145
  380.1 12.8 %all-to-all-done.8 = f32[64,1,4]{2,1,0:T(1,128)S(1)} async-done(((f32[64,1,4]{2,1,0:T(1,128)}), f32[64,1,4]{2,1,0:T(1,128)S(1)}, u32[]{:S(2)}, u32[]{:S(2)}) %all-to-all-start.8) | async-done | bytes 1056 | tf_op jit(solution)/shard_map/all_to_all | solution.py:145
  392.9 6.0 %all-to-all-start.5 = ((f32[8,1,192]{2,1,0:T(1,128)}), f32[8,1,192]{2,1,0:T(1,128)S(1)}, u32[]{:S(2)}, u32[]{:S(2)}) async-start(f32[8,1,192]{2,1,0:T(1,128)} %reshape.195), calls=%async_computation.5 | async-start | bytes 16384 | tf_op jit(solution)/shard_map/all_to_all | solution.py:138
  400.3 6.8 %gather_fusion.1 = f32[1024]{0:T(1024)S(1)} fusion(f32[256]{0:T(256)S(1)} %reshape.106, s32[1024]{0:T(1024)S(1)} %get-tuple-element.87), kind=kCustom, calls=%fused_computation.1 | custom fusion | bytes 12288 | tf_op jit(solution)/shard_map/jit(_take)/gather | solution.py:147
  408.8 6.2 %gather_fusion = f32[1024]{0:T(1024)S(1)} fusion(f32[1536]{0:T(1024)S(1)} %reshape.103, s32[1024]{0:T(1024)S(1)} %get-tuple-element.89), kind=kCustom, calls=%fused_computation | custom fusion | bytes 12288 | tf_op jit(solution)/shard_map/jit(_take)/gather | solution.py:146
  (83 shorter events, 56.9 us)
Async XLA Ops:
  6.5 49.5 %copy-start = (bf16[1024,1024]{1,0:T(8,128)(2,1)S(1)}, bf16[1024,1024]{1,0:T(8,128)(2,1)}, u32[]{:S(2)}) copy-start(bf16[1024,1024]{1,0:T(8,128)(2,1)} %param.4) | copy-start | bytes 6291460
  13.8 32.9 %all-to-all-start.6 = ((s32[64,1,4]{2,1,0:T(1,128)}), s32[64,1,4]{2,1,0:T(1,128)S(1)}, u32[]{:S(2)}, u32[]{:S(2)}) async-start(s32[64,1,4]{2,1,0:T(1,128)} %bitcast), calls=%async_computation.6 | async-start | bytes 65536 | tf_op jit(solution)/shard_map/all_to_all | solution.py:104
  46.7 24.4 %all-to-all-start = ((s32[64,8,3]{1,2,0:T(4,128)}), s32[64,8,3]{1,2,0:T(4,128)S(1)}, u32[]{:S(2)}, u32[]{:S(2)}) async-start(s32[64,8,3]{1,2,0:T(4,128)} %copy.16), calls=%async_computation | async-start | bytes 262144 | tf_op jit(solution)/shard_map/all_to_all | solution.py:95
  71.1 35.1 %all-to-all-start.7 = ((bf16[64,4,1024]{2,1,0:T(4,128)(2,1)}), bf16[64,4,1024]{2,1,0:T(4,128)(2,1)S(1)}, u32[]{:S(2)}, u32[]{:S(2)}) async-start(bf16[64,4,1024]{2,1,0:T(4,128)(2,1)} %reshape.104), calls=%async_computation.7 | async-start | bytes 1048576 | tf_op jit(solution)/shard_map/all_to_all | solution.py:103
  106.2 0.8 copy-start.2
  107.0 147.2 %all-to-all-start.2 = ((bf16[64,8,3,1024]{3,1,2,0:T(8,128)(2,1)}), bf16[64,8,3,1024]{3,1,2,0:T(8,128)(2,1)S(1)}, u32[]{:S(2)}, u32[]{:S(2)}) async-start(bf16[64,8,3,1024]{3,1,2,0:T(8,128)(2,1)} %copy.19), calls=%async_computation.2 | async-start | bytes 6291456 | tf_op jit(solution)/shard_map/all_to_all | solution.py:88
  116.0 202.9 %all-gather.3.cloned.1.call-start = ((), (), s32[]{:S(2)}) async-start(), calls=%async_computation.9 | async-start | bytes 4718592 | tf_op jit(solution)/shard_map/all_gather | solution.py:129
  254.3 16.7 %all-to-all-start.1 = ((s32[8,1,192]{2,1,0:T(1,128)}), s32[8,1,192]{2,1,0:T(1,128)S(1)}, u32[]{:S(2)}, u32[]{:S(2)}) async-start(s32[8,1,192]{2,1,0:T(1,128)} %reshape.193), calls=%async_computation.1 | async-start | bytes 16384 | tf_op jit(solution)/shard_map/all_to_all | solution.py:94
  271.0 52.3 %all-to-all-start.3 = ((bf16[64,8,3,1024]{3,0,2,1:T(8,128)(2,1)}), bf16[64,8,3,1024]{3,0,2,1:T(8,128)(2,1)S(1)}, u32[]{:S(2)}, u32[]{:S(2)}) async-start(bf16[64,8,3,1024]{3,0,2,1:T(8,128)(2,1)} %copy.20), calls=%async_computation.3 | async-start | bytes 6291456 | tf_op jit(solution)/shard_map/all_to_all | solution.py:87
  318.5 4.7 %copy-start.1 = (s32[64,8,3]{2,1,0:T(8,128)}, s32[64,8,3]{2,1,0:T(8,128)S(1)}, u32[]{:S(2)}) copy-start(s32[64,8,3]{2,1,0:T(8,128)S(1)} %copy.18) | copy-start | bytes 18436
  352.3 21.2 %all-to-all-start.4 = ((f32[64,8,3]{1,2,0:T(4,128)}), f32[64,8,3]{1,2,0:T(4,128)S(1)}, u32[]{:S(2)}, u32[]{:S(2)}) async-start(f32[64,8,3]{1,2,0:T(4,128)} %copy.23), calls=%async_computation.4 | async-start | bytes 262144 | tf_op jit(solution)/shard_map/all_to_all | solution.py:139
  373.5 19.4 %all-to-all-start.8 = ((f32[64,1,4]{2,1,0:T(1,128)}), f32[64,1,4]{2,1,0:T(1,128)S(1)}, u32[]{:S(2)}, u32[]{:S(2)}) async-start(f32[64,1,4]{2,1,0:T(1,128)} %bitcast.3), calls=%async_computation.8 | async-start | bytes 65536 | tf_op jit(solution)/shard_map/all_to_all | solution.py:145
  392.9 14.2 %all-to-all-start.5 = ((f32[8,1,192]{2,1,0:T(1,128)}), f32[8,1,192]{2,1,0:T(1,128)S(1)}, u32[]{:S(2)}, u32[]{:S(2)}) async-start(f32[8,1,192]{2,1,0:T(1,128)} %reshape.195), calls=%async_computation.5 | async-start | bytes 16384 | tf_op jit(solution)/shard_map/all_to_all | solution.py:138
Sparse Core Ops, SparseCore 0:
  119.0 42.0 all-gather.2
where the time goes:
time: 424 us; the launch traced here: 422 us
  waiting for transfers between devices  184 us (43%)
  starting transfers between devices  77.6 us (18%)
  local copies, waits for them, and re-layouts  66.6 us (16%)
  blocking collectives  39.7 us (9%)
  other arithmetic  24.9 us (6%)
  between operations  13.7 us (3%)
  matrix products  13.3 us (3%)
    all_to_all x1, waiting for transfers between devices, local(): lax.all_to_all(small_send, 'dp', split_axis=0, concat_axis=0, tiled=True)  136 us
    all_gather x1, blocking collectives, local(): piece_ids = lax.all_gather(spread_ids, 'sub', axis=0, tiled=True)  39.7 us
    all_to_all x1, starting transfers between devices, local(): lax.all_to_all(large_tags, 'dp', split_axis=0, concat_axis=0, tiled=True)  19.3 us
    all_to_all x1, waiting for transfers between devices, local(): lax.all_to_all(planned_density, 'dp', split_axis=0, concat_axis=0, tiled=...  15 us
    reshape x2, local copies, waits for them, and re-layouts, local(): small_send.reshape(dp_count, sub_count, small_cap, feature_width)  14.7 us
    dot_general x4, matrix products, pair_terms(): lax.dot_general(left_rows, right_rows, (((1,), (1,)), ((), ())), preferre...  13.3 us
    all_to_all x1, waiting for transfers between devices, local(): lax.all_to_all(spread_density, 'dp', split_axis=0, concat_axis=0, tiled=T...  12.8 us
    all_to_all x1, starting transfers between devices, local(): lax.all_to_all(lax.all_to_all(small_tags, 'dp', split_axis=0, concat_axis...  12.1 us
  transfers between devices with their start and end apart: 10, of which 7 were waited for; matrix products, arithmetic and copies ran while one was open for 15% of the time, Pallas kernels for 0%

commit v1 on v0

--- a/solution.py
+++ b/solution.py
@@ -6,6 +6,17 @@
 SC = 2
 LC = 1
 kernel_scale = 32.0
+
+
+def around_the_ring(value, name, dim):
+    size = lax.axis_size(name)
+    route = [(i, (i + 1) % size) for i in range(size)]
+    blocks = [value]
+    for hop in range(1, size):
+        blocks = [lax.ppermute(blocks[0], name, route), *blocks]
+    whole = jnp.concatenate(blocks, axis=dim)
+    shift = (lax.axis_index(name) + 1) * blocks[-1].shape[dim]
+    return jnp.roll(whole, shift, axis=dim)
 
 
 def unit_norm(values):
@@ -127,7 +138,7 @@
     places = jnp.arange(spread_total, dtype=jnp.int32)
     my_places = lax.axis_index("sub") * spread_total + places
     piece_rows = lax.all_gather(spread_flat, "sub", axis=0, tiled=True)
-    piece_ids = lax.all_gather(spread_ids, "sub", axis=0, tiled=True)
+    piece_ids = around_the_ring(spread_ids, "sub", 0)
     piece_places = jnp.arange(piece_rows.shape[0], dtype=jnp.int32)
     weights, same_cluster = pair_terms(
         spread_flat, spread_ids, my_places, piece_rows, piece_ids, piece_places

time: 424 us -> 416 us (0.981)
  blocking collectives: 39.7 us -> 0 us
  waiting for transfers between devices: 184 us -> 204 us
  starting transfers between devices: 77.6 us -> 90.2 us
    all_gather x1 -> x0, blocking collectives: 39.7 us -> none  [local(): piece_ids = lax.all_gather(spread_ids, 'sub', axis=0, tiled=True)]
    all_to_all x1, waiting for transfers between devices: 0.01 us -> 30.5 us  [local(): lax.all_to_all(lax.all_to_all(small_send, 'dp', split_axis=0, concat_axis...]
    all_to_all x1, waiting for transfers between devices: 136 us -> 119 us  [local(): lax.all_to_all(small_send, 'dp', split_axis=0, concat_axis=0, tiled=True)]
    ppermute x0 -> x7, starting transfers between devices: none -> 12.3 us  [around_the_ring(): blocks = [lax.ppermute(blocks[0], name, route), *blocks]]
    ppermute x0 -> x7, waiting for transfers between devices: none -> 7.33 us  [around_the_ring(): blocks = [lax.ppermute(blocks[0], name, route), *blocks]]
  transfers between devices with their start and end apart: 10 -> 17, of which waited for: 7 -> 12; matrix products, arithmetic and copies ran while one was open for 15% -> 15% of each run, Pallas kernels for 0% -> 0%
where the time goes in v1:
time: 416 us; the launch traced here: 415 us
  waiting for transfers between devices  204 us (49%)
  starting transfers between devices  90.2 us (22%)
  local copies, waits for them, and re-layouts  66.6 us (16%)
  other arithmetic  24.9 us (6%)
  between operations  13.8 us (3%)
  matrix products  13.3 us (3%)
    all_to_all x1, waiting for transfers between devices, local(): lax.all_to_all(small_send, 'dp', split_axis=0, concat_axis=0, tiled=True)  119 us
    all_to_all x1, waiting for transfers between devices, local(): lax.all_to_all(lax.all_to_all(small_send, 'dp', split_axis=0, concat_axis...  30.5 us
    all_to_all x1, starting transfers between devices, local(): lax.all_to_all(large_tags, 'dp', split_axis=0, concat_axis=0, tiled=True)  19.3 us
    reshape x2, local copies, waits for them, and re-layouts, local(): small_send.reshape(dp_count, sub_count, small_cap, feature_width)  14.7 us
    all_to_all x1, waiting for transfers between devices, local(): lax.all_to_all(planned_density, 'dp', split_axis=0, concat_axis=0, tiled=...  14.6 us
    dot_general x4, matrix products, pair_terms(): lax.dot_general(left_rows, right_rows, (((1,), (1,)), ((), ())), preferre...  13.3 us
    all_to_all x1, waiting for transfers between devices, local(): lax.all_to_all(spread_density, 'dp', split_axis=0, concat_axis=0, tiled=T...  12.8 us
    ppermute x7, starting transfers between devices, around_the_ring(): blocks = [lax.ppermute(blocks[0], name, route), *blocks]  12.3 us
  transfers between devices with their start and end apart: 17, of which 12 were waited for; matrix products, arithmetic and copies ran while one was open for 15% of the time, Pallas kernels for 0%

profile of v1, /device:TPU:1, one launch (start us, length us, event | category | flops | bytes accessed | tf_op | source)
XLA Modules:
  0.0 415.2 jit_solution(3953129715769482599)
XLA Ops:
  13.8 19.3 %all-to-all-start.6 = ((s32[64,1,4]{2,1,0:T(1,128)}), s32[64,1,4]{2,1,0:T(1,128)S(1)}, u32[]{:S(2)}, u32[]{:S(2)}) async-start(s32[64,1,4]{2,1,0:T(1,128)} %bitcast), calls=%async_computation.6 | async-start | bytes 65536 | tf_op jit(solution)/shard_map/all_to_all | solution.py:115
  41.5 5.2 %all-to-all-done.6 = s32[64,1,4]{2,1,0:T(1,128)S(1)} async-done(((s32[64,1,4]{2,1,0:T(1,128)}), s32[64,1,4]{2,1,0:T(1,128)S(1)}, u32[]{:S(2)}, u32[]{:S(2)}) %all-to-all-start.6) | async-done | bytes 1056 | tf_op jit(solution)/shard_map/all_to_all | solution.py:115
  46.7 9.3 %all-to-all-start = ((s32[64,8,3]{1,2,0:T(4,128)}), s32[64,8,3]{1,2,0:T(4,128)S(1)}, u32[]{:S(2)}, u32[]{:S(2)}) async-start(s32[64,8,3]{1,2,0:T(4,128)} %copy.16), calls=%async_computation | async-start | bytes 262144 | tf_op jit(solution)/shard_map/all_to_all | solution.py:106
  56.0 5.7 %scatter_custom_fusion.3 = bf16[256,1024]{1,0:T(8,128)(2,1)S(1)} fusion(s32[1024]{0:T(1024)S(1)} %get-tuple-element.88, bf16[1024,1024]{1,0:T(8,128)(2,1)S(1)} %copy-done, f32[1024]{0:T(1024)S(1)} %add_rsqrt_fusion, bf16[]{:T(256)} %constant.108.clone.1), kind=kCustom, calls=%fused_computation.40 | custom fusion | flops 3145728 | bytes 2625538 | tf_op jit(solution)/shard_map/scatter | solution.py:90
  62.7 8.4 %all-to-all-done = s32[64,8,3]{1,2,0:T(4,128)S(1)} async-done(((s32[64,8,3]{1,2,0:T(4,128)}), s32[64,8,3]{1,2,0:T(4,128)S(1)}, u32[]{:S(2)}, u32[]{:S(2)}) %all-to-all-start) | async-done | bytes 6176 | tf_op jit(solution)/shard_map/all_to_all | solution.py:106
  71.1 6.4 %all-to-all-start.7 = ((bf16[64,4,1024]{2,1,0:T(4,128)(2,1)}), bf16[64,4,1024]{2,1,0:T(4,128)(2,1)S(1)}, u32[]{:S(2)}, u32[]{:S(2)}) async-start(bf16[64,4,1024]{2,1,0:T(4,128)(2,1)} %reshape.104), calls=%async_computation.7 | async-start | bytes 1048576 | tf_op jit(solution)/shard_map/all_to_all | solution.py:114
  77.5 7.8 %scatter_custom_fusion.1 = bf16[1536,1024]{1,0:T(8,128)(2,1)} fusion(s32[1024]{0:T(1024)S(1)} %get-tuple-element.90, bf16[]{:T(256)} %constant.108.clone.1, bf16[1024,1024]{1,0:T(8,128)(2,1)S(1)} %copy-done, f32[1024]{0:T(1024)S(1)} %add_rsqrt_fusion), kind=kCustom, calls=%fused_computation.37 | custom fusion | flops 3145728 | bytes 5246978 | tf_op jit(solution)/shard_map/scatter | solution.py:78
  85.3 9.1 %reshape.100 = bf16[64,8,3,1024]{3,2,1,0:T(4,128)(2,1)} reshape(bf16[1536,1024]{1,0:T(8,128)(2,1)} %scatter_custom_fusion.1) | data formatting | bytes 6291456 | tf_op jit(solution)/shard_map/reshape | solution.py:80
  94.4 5.6 %copy.19 = bf16[64,8,3,1024]{3,1,2,0:T(8,128)(2,1)} copy(bf16[64,8,3,1024]{3,2,1,0:T(4,128)(2,1)} %reshape.100) | data formatting | bytes 6291456 | tf_op jit(solution)/shard_map/reshape | solution.py:80
  100.0 6.3 %all-to-all-done.7 = bf16[64,4,1024]{2,1,0:T(4,128)(2,1)S(1)} async-done(((bf16[64,4,1024]{2,1,0:T(4,128)(2,1)}), bf16[64,4,1024]{2,1,0:T(4,128)(2,1)S(1)}, u32[]{:S(2)}, u32[]{:S(2)}) %all-to-all-start.7) | async-done | bytes 524320 | tf_op jit(solution)/shard_map/all_to_all | solution.py:114
  107.0 8.9 %all-to-all-start.2 = ((bf16[64,8,3,1024]{3,1,2,0:T(8,128)(2,1)}), bf16[64,8,3,1024]{3,1,2,0:T(8,128)(2,1)S(1)}, u32[]{:S(2)}, u32[]{:S(2)}) async-start(bf16[64,8,3,1024]{3,1,2,0:T(8,128)(2,1)} %copy.19), calls=%async_computation.2 | async-start | bytes 6291456 | tf_op jit(solution)/shard_map/all_to_all | solution.py:99
  135.2 119.1 %all-to-all-done.2 = bf16[64,8,3,1024]{3,1,2,0:T(8,128)(2,1)S(1)} async-done(((bf16[64,8,3,1024]{3,1,2,0:T(8,128)(2,1)}), bf16[64,8,3,1024]{3,1,2,0:T(8,128)(2,1)S(1)}, u32[]{:S(2)}, u32[]{:S(2)}) %all-to-all-start.2) | async-done | bytes 3145760 | tf_op jit(solution)/shard_map/all_to_all | solution.py:99
  254.3 12.1 %all-to-all-start.1 = ((s32[8,1,192]{2,1,0:T(1,128)}), s32[8,1,192]{2,1,0:T(1,128)S(1)}, u32[]{:S(2)}, u32[]{:S(2)}) async-start(s32[8,1,192]{2,1,0:T(1,128)} %reshape.187), calls=%async_computation.1 | async-start | bytes 16384 | tf_op jit(solution)/shard_map/all_to_all | solution.py:105
  285.6 30.5 %all-to-all-done.3 = bf16[64,8,3,1024]{3,0,2,1:T(8,128)(2,1)S(1)} async-done(((bf16[64,8,3,1024]{3,0,2,1:T(8,128)(2,1)}), bf16[64,8,3,1024]{3,0,2,1:T(8,128)(2,1)S(1)}, u32[]{:S(2)}, u32[]{:S(2)}) %all-to-all-start.3) | async-done | bytes 3145760 | tf_op jit(solution)/shard_map/all_to_all | solution.py:98
  316.1 4.6 %copy.21 = bf16[64,8,3,1024]{3,2,1,0:T(4,128)(2,1)} copy(bf16[64,8,3,1024]{3,0,2,1:T(8,128)(2,1)S(1)} %all-to-all-done.3) | data formatting | bytes 6291456 | tf_op jit(solution)/shard_map/all_to_all | solution.py:98
  320.7 7.5 %reshape.101 = bf16[1536,1024]{1,0:T(8,128)(2,1)S(1)} reshape(bf16[64,8,3,1024]{3,2,1,0:T(4,128)(2,1)} %copy.21) | data formatting | bytes 6291456 | tf_op jit(solution)/shard_map/reshape | solution.py:117
  328.3 15.6 %while.12 = (s32[]{:T(128)}, f32[3,512]{1,0:T(4,128)S(1)}, s32[3]{0:T(128)S(1)}, s32[1536]{0:T(1024)S(1)}, s32[64,8,3]{2,1,0:T(8,128)}, /*index=5*/bf16[1536,102...) while((s32[]{:T(128)}, f32[3,512]{1,0:T(4,128)S(1)}, ...), condition=%wide.wide.region_7.8_spmd.clone, body=%wide.wide.region_4.7_spmd.clone.sunk | while | flops 1619265024 | bytes 4237495 | solution.py:133
  345.2 5.6 %all-to-all-start.4 = ((f32[64,8,3]{1,2,0:T(4,128)}), f32[64,8,3]{1,2,0:T(4,128)S(1)}, u32[]{:S(2)}, u32[]{:S(2)}) async-start(f32[64,8,3]{1,2,0:T(4,128)} %copy.23), calls=%async_computation.4 | async-start | bytes 262144 | tf_op jit(solution)/shard_map/all_to_all | solution.py:150
  351.4 14.6 %all-to-all-done.4 = f32[64,8,3]{1,2,0:T(4,128)S(1)} async-done(((f32[64,8,3]{1,2,0:T(4,128)}), f32[64,8,3]{1,2,0:T(4,128)S(1)}, u32[]{:S(2)}, u32[]{:S(2)}) %all-to-all-start.4) | async-done | bytes 6176 | tf_op jit(solution)/shard_map/all_to_all | solution.py:150
  365.9 6.1 %all-to-all-start.8 = ((f32[64,1,4]{2,1,0:T(1,128)}), f32[64,1,4]{2,1,0:T(1,128)S(1)}, u32[]{:S(2)}, u32[]{:S(2)}) async-start(f32[64,1,4]{2,1,0:T(1,128)} %bitcast.2), calls=%async_computation.8 | async-start | bytes 65536 | tf_op jit(solution)/shard_map/all_to_all | solution.py:156
  372.9 12.8 %all-to-all-done.8 = f32[64,1,4]{2,1,0:T(1,128)S(1)} async-done(((f32[64,1,4]{2,1,0:T(1,128)}), f32[64,1,4]{2,1,0:T(1,128)S(1)}, u32[]{:S(2)}, u32[]{:S(2)}) %all-to-all-start.8) | async-done | bytes 1056 | tf_op jit(solution)/shard_map/all_to_all | solution.py:156
  385.7 6.0 %all-to-all-start.5 = ((f32[8,1,192]{2,1,0:T(1,128)}), f32[8,1,192]{2,1,0:T(1,128)S(1)}, u32[]{:S(2)}, u32[]{:S(2)}) async-start(f32[8,1,192]{2,1,0:T(1,128)} %reshape.189), calls=%async_computation.5 | async-start | bytes 16384 | tf_op jit(solution)/shard_map/all_to_all | solution.py:149
  393.1 6.8 %gather_fusion.1 = f32[1024]{0:T(1024)S(1)} fusion(f32[256]{0:T(256)S(1)} %reshape.106, s32[1024]{0:T(1024)S(1)} %get-tuple-element.87), kind=kCustom, calls=%fused_computation.1 | custom fusion | bytes 12288 | tf_op jit(solution)/shard_map/jit(_take)/gather | solution.py:158
  401.6 6.2 %gather_fusion = f32[1024]{0:T(1024)S(1)} fusion(f32[1536]{0:T(1024)S(1)} %reshape.103, s32[1024]{0:T(1024)S(1)} %get-tuple-element.89), kind=kCustom, calls=%fused_computation | custom fusion | bytes 12288 | tf_op jit(solution)/shard_map/jit(_take)/gather | solution.py:157
  (113 shorter events, 75.3 us)
Async XLA Ops:
  6.5 49.5 %copy-start = (bf16[1024,1024]{1,0:T(8,128)(2,1)S(1)}, bf16[1024,1024]{1,0:T(8,128)(2,1)}, u32[]{:S(2)}) copy-start(bf16[1024,1024]{1,0:T(8,128)(2,1)} %param.4) | copy-start | bytes 6291460
  13.8 32.9 %all-to-all-start.6 = ((s32[64,1,4]{2,1,0:T(1,128)}), s32[64,1,4]{2,1,0:T(1,128)S(1)}, u32[]{:S(2)}, u32[]{:S(2)}) async-start(s32[64,1,4]{2,1,0:T(1,128)} %bitcast), calls=%async_computation.6 | async-start | bytes 65536 | tf_op jit(solution)/shard_map/all_to_all | solution.py:115
  46.7 24.4 %all-to-all-start = ((s32[64,8,3]{1,2,0:T(4,128)}), s32[64,8,3]{1,2,0:T(4,128)S(1)}, u32[]{:S(2)}, u32[]{:S(2)}) async-start(s32[64,8,3]{1,2,0:T(4,128)} %copy.16), calls=%async_computation | async-start | bytes 262144 | tf_op jit(solution)/shard_map/all_to_all | solution.py:106
  71.1 35.1 %all-to-all-start.7 = ((bf16[64,4,1024]{2,1,0:T(4,128)(2,1)}), bf16[64,4,1024]{2,1,0:T(4,128)(2,1)S(1)}, u32[]{:S(2)}, u32[]{:S(2)}) async-start(bf16[64,4,1024]{2,1,0:T(4,128)(2,1)} %reshape.104), calls=%async_computation.7 | async-start | bytes 1048576 | tf_op jit(solution)/shard_map/all_to_all | solution.py:114
  106.2 0.8 copy-start.2
  107.0 147.2 %all-to-all-start.2 = ((bf16[64,8,3,1024]{3,1,2,0:T(8,128)(2,1)}), bf16[64,8,3,1024]{3,1,2,0:T(8,128)(2,1)S(1)}, u32[]{:S(2)}, u32[]{:S(2)}) async-start(bf16[64,8,3,1024]{3,1,2,0:T(8,128)(2,1)} %copy.19), calls=%async_computation.2 | async-start | bytes 6291456 | tf_op jit(solution)/shard_map/all_to_all | solution.py:99
  116.0 165.3 %all-gather.2.cloned.1.call-start = ((), (), s32[]{:S(2)}) async-start(), calls=%async_computation.9 | async-start | bytes 4718592 | tf_op jit(solution)/shard_map/all_gather | solution.py:140
  119.3 3.6 collective-permute-start
  122.9 3.0 collective-permute-start.1
  126.0 4.2 %collective-permute-start.2 = (s32[256]{0:T(256)S(1)}, s32[256]{0:T(256)S(1)}, u32[]{:S(2)}, u32[]{:S(2)}) collective-permute-start(s32[256]{0:T(256)S(1)} %collective-permute-done.1), channel_id=1, source_target_pairs={{0,1},{1,2},{2,3},{3,4},{4,5},{5,6},{6,7},{7,0},{8,9},{9,10},{10,1... | collective-permute-start | bytes 3080 | tf_op jit(solution)/shard_map/ppermute | solution.py:16
  130.2 4.2 %collective-permute-start.3 = (s32[256]{0:T(256)S(1)}, s32[256]{0:T(256)S(1)}, u32[]{:S(2)}, u32[]{:S(2)}) collective-permute-start(s32[256]{0:T(256)S(1)} %collective-permute-done.2), channel_id=1, source_target_pairs={{0,1},{1,2},{2,3},{3,4},{4,5},{5,6},{6,7},{7,0},{8,9},{9,10},{10,1... | collective-permute-start | bytes 3080 | tf_op jit(solution)/shard_map/ppermute | solution.py:16
  134.4 132.0 %collective-permute-start.4 = (s32[256]{0:T(256)S(1)}, s32[256]{0:T(256)S(1)}, u32[]{:S(2)}, u32[]{:S(2)}) collective-permute-start(s32[256]{0:T(256)S(1)} %collective-permute-done.3), channel_id=1, source_target_pairs={{0,1},{1,2},{2,3},{3,4},{4,5},{5,6},{6,7},{7,0},{8,9},{9,10},{10,1... | collective-permute-start | bytes 3080 | tf_op jit(solution)/shard_map/ppermute | solution.py:16
  254.3 20.2 %all-to-all-start.1 = ((s32[8,1,192]{2,1,0:T(1,128)}), s32[8,1,192]{2,1,0:T(1,128)S(1)}, u32[]{:S(2)}, u32[]{:S(2)}) async-start(s32[8,1,192]{2,1,0:T(1,128)} %reshape.187), calls=%async_computation.1 | async-start | bytes 16384 | tf_op jit(solution)/shard_map/all_to_all | solution.py:105
  266.4 2.4 collective-permute-start.5
  268.8 9.8 %collective-permute-start.6 = (s32[256]{0:T(256)S(1)}, s32[256]{0:T(256)S(1)}, u32[]{:S(2)}, u32[]{:S(2)}) collective-permute-start(s32[256]{0:T(256)S(1)} %collective-permute-done.5), channel_id=1, source_target_pairs={{0,1},{1,2},{2,3},{3,4},{4,5},{5,6},{6,7},{7,0},{8,9},{9,10},{10,1... | collective-permute-start | bytes 3080 | tf_op jit(solution)/shard_map/ppermute | solution.py:16
  274.4 41.7 %all-to-all-start.3 = ((bf16[64,8,3,1024]{3,0,2,1:T(8,128)(2,1)}), bf16[64,8,3,1024]{3,0,2,1:T(8,128)(2,1)S(1)}, u32[]{:S(2)}, u32[]{:S(2)}) async-start(bf16[64,8,3,1024]{3,0,2,1:T(8,128)(2,1)} %copy.20), calls=%async_computation.3 | async-start | bytes 6291456 | tf_op jit(solution)/shard_map/all_to_all | solution.py:98
  280.8 4.7 %copy-start.1 = (s32[64,8,3]{2,1,0:T(8,128)}, s32[64,8,3]{2,1,0:T(8,128)S(1)}, u32[]{:S(2)}) copy-start(s32[64,8,3]{2,1,0:T(8,128)S(1)} %copy.18) | copy-start | bytes 18436
  345.2 20.8 %all-to-all-start.4 = ((f32[64,8,3]{1,2,0:T(4,128)}), f32[64,8,3]{1,2,0:T(4,128)S(1)}, u32[]{:S(2)}, u32[]{:S(2)}) async-start(f32[64,8,3]{1,2,0:T(4,128)} %copy.23), calls=%async_computation.4 | async-start | bytes 262144 | tf_op jit(solution)/shard_map/all_to_all | solution.py:150
  365.9 19.8 %all-to-all-start.8 = ((f32[64,1,4]{2,1,0:T(1,128)}), f32[64,1,4]{2,1,0:T(1,128)S(1)}, u32[]{:S(2)}, u32[]{:S(2)}) async-start(f32[64,1,4]{2,1,0:T(1,128)} %bitcast.2), calls=%async_computation.8 | async-start | bytes 65536 | tf_op jit(solution)/shard_map/all_to_all | solution.py:156
  385.7 14.2 %all-to-all-start.5 = ((f32[8,1,192]{2,1,0:T(1,128)}), f32[8,1,192]{2,1,0:T(1,128)S(1)}, u32[]{:S(2)}, u32[]{:S(2)}) async-start(f32[8,1,192]{2,1,0:T(1,128)} %reshape.189), calls=%async_computation.5 | async-start | bytes 16384 | tf_op jit(solution)/shard_map/all_to_all | solution.py:149
Sparse Core Ops, SparseCore 0:
  119.0 42.0 all-gather.1
